TPU v7x, 512 devices: a whole 4x8x8 slice. The times are simulated.
512 devices in a mesh: grp: 16 (over y, x_hi), blk: 32 (over x_lo, z, core).
Axes of the slice: x: 4 (x_hi: 2, x_lo: 2; x = x_hi * 2 + x_lo), y: 8, z: 8, core: 2. Of those that a mesh axis runs over, the one named last changes fastest.
Arguments:
- sigma_anc: float32 [16384, 16384], P('grp', 'blk')
- panels: float32 [16384, 1024], P(('grp', 'blk')), may hold values from -0.0625 to 0.0625
- diag_inv: float32 [1024, 256], replicated, may hold values from -6 to 6
- scaled_parent_panel: float32 [512, 256], replicated, may hold values from -0.375 to 0.375
- struct_upper: int32 [2, 32], replicated, may hold values from 0 to 63, as said below
- struct_lower: int32 [2, 16], replicated, may hold values from 0 to 63, as said below
Outputs:
- cov_panel: float32 [16384, 1024], P(('blk', 'grp'))
- cov_diag: float32 [1024, 256], P('blk')
- cov_parent: float32 [512, 256], P('blk')
Inputs may be any that keep to these rules, and one draw needn't show every extreme that they name: `struct_upper`: each row lists 32 different ancestor blocks. `struct_lower`: each row lists 16 different blocks, all in its parent's row of struct_upper.
All inputs are finite; a program needn't handle non-finite values.
Results may differ from a plain program's by a relative error of at most 0.00011.
Values sent between devices are 32-bit elements; how exact they have to be, the bound alone decides.
A program may use at most 64 MiB of HBM per device.

v0:
```python
import jax
import jax.numpy as jnp
from jax import lax
from jax.sharding import PartitionSpec as P

W = 256
HIGH = lax.Precision.HIGH
HIGHEST = lax.Precision.HIGHEST


def dot(a, b, ca, cb, precision=HIGH):
    return lax.dot_general(
        a, b, (((ca,), (cb,)), ((), ())), precision=precision, preferred_element_type=jnp.float32
    )


def listed(struct_upper, struct_lower, block):
    upper = jnp.any(struct_upper == block, axis=1)
    lower = jnp.any(struct_lower == block, axis=1)
    flags = jnp.concatenate([upper, lower]).astype(jnp.float32)
    return jnp.repeat(flags, W)[None, :]


def gather_rows(rows):
    return lax.all_gather(rows, "blk", axis=0, tiled=True)


def scatter_products(partial):
    return lax.psum_scatter(partial, "grp", scatter_dimension=0, tiled=True)


def sum_blocks(terms):
    return lax.psum(lax.psum_scatter(terms, "blk", scatter_dimension=0, tiled=True), "grp")


def per_device(sigma_anc, panels, diag_inv, scaled_parent_panel, struct_upper, struct_lower):
    grp = lax.axis_index("grp")
    blk = lax.axis_index("blk")
    v = [scaled_parent_panel[:W], scaled_parent_panel[W:]]
    u = panels * listed(struct_upper, struct_lower, (grp * 32 + blk) // 8)
    x = [
        dot(u[:, c * W : (c + 1) * W], v[c], 1, 0) - u[:, (c + 2) * W : (c + 3) * W] for c in (0, 1)
    ]
    w = jnp.concatenate([u[:, : 2 * W], x[0], x[1]], axis=1)
    moves = [(q, q % 16 * 32 + q // 16) for q in range(512)]
    w_own = lax.ppermute(w, ("grp", "blk"), moves)
    gathered = gather_rows(w)
    t = scatter_products(dot(sigma_anc, gathered, 0, 0))
    own = listed(struct_upper, struct_lower, (blk * 16 + grp) // 8)
    sign = jnp.where(jnp.arange(4 * W) < 2 * W, -1.0, 1.0).astype(jnp.float32)[None, :]
    cov_panel = t * (own * sign)

    def part(a, i):
        return a[:, i * W : (i + 1) * W]

    diag_terms = [dot(part(w_own, i), part(t, i), 0, 0) for i in range(4)]
    parent_terms = [dot(part(w_own, c), part(t, c + 2), 0, 0) for c in (0, 1)]
    terms = jnp.concatenate(
        [
            jnp.concatenate(diag_terms, axis=0).reshape(32, 32, W),
            jnp.concatenate(parent_terms, axis=0).reshape(32, 16, W),
        ],
        axis=1,
    ).reshape(32 * 48, W)
    base_parent = [dot(diag_inv[c * W : (c + 1) * W], v[c], 1, 0, HIGHEST) for c in (0, 1)]
    base_low = [dot(v[c], base_parent[c], 0, 0, HIGHEST) for c in (0, 1)]
    zero = jnp.zeros((2 * W, W), jnp.float32)
    base_diag = diag_inv + jnp.concatenate([zero] + base_low, axis=0)
    base_parent = jnp.concatenate(base_parent, axis=0)
    summed = sum_blocks(terms)
    cov_diag = lax.dynamic_slice_in_dim(base_diag, blk * 32, 32, 0) + summed[:32]
    cov_parent = -(lax.dynamic_slice_in_dim(base_parent, blk * 16, 16, 0) + summed[32:])
    return (cov_panel, cov_diag, cov_parent)


def solution(mesh):
    return jax.shard_map(
        per_device,
        mesh=mesh,
        in_specs=(P("grp", "blk"), P(("grp", "blk"), None), P(), P(), P(), P()),
        out_specs=(P(("blk", "grp"), None), P("blk", None), P("blk", None)),
        check_vma=False,
    )
```

profile of v0, /device:TPU:2, one launch (start us, length us, event | category | flops | bytes accessed | tf_op | source)
XLA Modules:
  0.0 522.6 jit_solution(6177603634470408080)
XLA Ops:
  7.3 1.0 compare_reduce_fusion.1
  8.2 0.8 compare_reduce_fusion
  9.2 0.9 broadcast_multiply_fusion.1
  10.1 1.2 convolution_subtract_fusion
  11.3 1.2 convolution_subtract_fusion.1
  12.5 0.7 pad_maximum_fusion.3
  13.2 73.8 %all-gather.2.cloned.1.call-done = f32[1024,1024]{1,0:T(8,128)} async-done(((f32[32,1024]{1,0:T(8,128)}), f32[1024,1024]{1,0:T(8,128)}) %all-gather.2.cloned.1.call-update) | async-done | bytes 4194320 | tf_op jit(solution)/shard_map/all_gather | solution.py:25
  87.0 7.0 %convolution_bitcast_fusion = f32[512,1024]{0,1:T(8,128)} fusion(f32[1024,1024]{1,0:T(8,128)} %all-gather.2.cloned.1.call-done, f32[1024,512]{1,0:T(8,128)S(1)} %copy-done), kind=kOutput, calls=%fused_computation | convolution fusion | flops 3221225472 | bytes 8388608 | tf_op jit(solution)/shard_map/dot_general | solution.py:12
  94.0 2.9 copy.11
  97.0 0.8 copy-done.3
  97.8 2.9 collective-permute-start
  100.7 210.4 %reduce-scatter.7.cloned.1.call-done = f32[32,1024]{1,0:T(8,128)} async-done(((f32[512,1024]{1,0:T(8,128)}), f32[32,1024]{1,0:T(8,128)}) %reduce-scatter.7.cloned.1.call-update) | async-done | bytes 131088
  311.1 1.1 copy.12
  312.2 0.3 fusion.14
  314.3 1.3 pad_maximum_fusion
  315.7 1.3 fusion
  317.1 1.3 fusion.2
  318.4 1.3 convolution_bitcast_fusion.1
  319.7 1.3 convolution_bitcast_fusion.2
  321.2 0.8 copy.10
  322.1 114.9 %reduce-scatter.5.cloned.1.call-done = f32[48,256]{1,0:T(8,128)} async-done(((f32[1536,256]{1,0:T(8,128)}), f32[48,256]{1,0:T(8,128)}) %reduce-scatter.5.cloned.1.call-update) | async-done | bytes 49168 | tf_op jit(solution)/shard_map/reduce_scatter | solution.py:33
  437.0 77.1 %psum.7 = f32[48,256]{1,0:T(8,128)S(1)} all-reduce(f32[48,256]{1,0:T(8,128)} %reduce-scatter.5.cloned.1.call-done), channel_id=1, replica_groups=mesh['grp'=16,'blk'=32] {'grp'}, use_global_device_ids=true, to_apply=%region_6.7 | all-reduce | flops 12288 | bytes 98304 | tf_op jit(solution)/shard_map/psum | solution.py:33
  514.0 0.6 fusion.32
  514.6 1.5 slice_add_fusion
  (31 shorter events, 2.4 us)
Async XLA Ops:
  7.2 79.8 %copy-start = (f32[1024,512]{1,0:T(8,128)S(1)}, f32[1024,512]{1,0:T(8,128)}, u32[]{:S(2)}) copy-start(f32[1024,512]{1,0:T(8,128)} %param.6) | copy-start | bytes 6291460
  7.2 79.8 %all-gather.2.cloned.1.call-start = ((), (), s32[]{:S(2)}) async-start(), calls=%async_computation.2 | async-start | bytes 4325376 | tf_op jit(solution)/shard_map/all_gather | solution.py:25
  13.2 297.9 %reduce-scatter.7.cloned.1.call-start = ((), (), s32[]{:S(2)}) async-start(), calls=%async_computation.4 | async-start | bytes 2228224
  96.9 0.9 copy-start.3
  96.9 340.0 %reduce-scatter.5.cloned.1.call-start = ((), (), s32[]{:S(2)}) async-start(), calls=%async_computation.3 | async-start | bytes 1622016 | tf_op jit(solution)/shard_map/reduce_scatter | solution.py:33
  97.8 214.3 %collective-permute-start = (f32[32,1024]{1,0:T(8,128)S(1)}, f32[32,1024]{1,0:T(8,128)S(1)}, u32[]{:S(2)}, u32[]{:S(2)}) collective-permute-start(f32[32,1024]{1,0:T(8,128)S(1)} %copy-done.3), channel_id=1, source_target_pairs={{0,0},{1,32},{2,64},{3,96},{4,128},{5,160},{6,192},{7,224},{8,256}... | collective-permute-start | bytes 393224 | tf_op jit(solution)/shard_map/ppermute | solution.py:46
  314.3 1.5 copy-start.1
  318.4 1.3 copy-start.2
Sparse Core Ops, SparseCore 0:
  13.3 73.6 all-gather.1
  97.1 213.9 reduce-scatter.6
  315.7 121.2 reduce-scatter.4
where the time goes:
time: 523 us
  waiting for transfers between devices  399 us (76%)
  blocking collectives  77.1 us (15%)
  matrix products  16.5 us (3%)
  between operations  13.9 us (3%)
  other arithmetic  7.11 us (1%)
  local copies, waits for them, and re-layouts  5.96 us (1%)
    unnamed x4, waiting for transfers between devices  210 us
    reduce_scatter x1, waiting for transfers between devices, sum_blocks(): lax.psum_scatter(terms, 'blk', scatter_dimension=0, tiled=True)  115 us
    psum x1, blocking collectives, sum_blocks(): lax.psum(lax.psum_scatter(terms, 'blk', scatter_dimension=0, tiled=True),...  77.1 us
    all_gather x1, waiting for transfers between devices, gather_rows(): return lax.all_gather(rows, 'blk', axis=0, tiled=True)  73.8 us
    dot_general x13, matrix products, dot(): lax.dot_general(a, b, (((ca,), (cb,)), ((), ())), precision=precision, pr...  16.5 us
  transfers between devices with their start and end apart: 4, of which 3 were waited for; matrix products, arithmetic and copies ran while one was open for 1% of the time, Pallas kernels for 0%

commit v1 on v0

--- a/solution.py
+++ b/solution.py
@@ -30,7 +30,10 @@
 
 
 def sum_blocks(terms):
-    return lax.psum(lax.psum_scatter(terms, "blk", scatter_dimension=0, tiled=True), "grp")
+    return jnp.sum(
+        lax.all_gather(lax.psum_scatter(terms, "blk", scatter_dimension=0, tiled=True), "grp"),
+        axis=0,
+    )
 
 
 def per_device(sigma_anc, panels, diag_inv, scaled_parent_panel, struct_upper, struct_lower):

time: 523 us -> 491 us (0.939)
  blocking collectives: 77.1 us -> 44.9 us
    psum x1 -> x0, blocking collectives: 77.1 us -> none  [sum_blocks(): lax.psum(lax.psum_scatter(terms, 'blk', scatter_dimension=0, tiled=True),...]
    all_gather x0 -> x1, blocking collectives: none -> 44.9 us  [sum_blocks(): lax.all_gather(lax.psum_scatter(terms, 'blk', scatter_dimension=0, tiled=...]
  transfers between devices with their start and end apart: 4 -> 4, of which waited for: 3 -> 3; matrix products, arithmetic and copies ran while one was open for 1% -> 2% of each run, Pallas kernels for 0% -> 0%
where the time goes in v1:
time: 491 us
  waiting for transfers between devices  397 us (81%)
  blocking collectives  44.9 us (9%)
  matrix products  16.5 us (3%)
  between operations  13.9 us (3%)
  other arithmetic  7.98 us (2%)
  local copies, waits for them, and re-layouts  7 us (1%)
    unnamed x4, waiting for transfers between devices  210 us
    reduce_scatter x1, waiting for transfers between devices, sum_blocks(): lax.psum_scatter(terms, 'blk', scatter_dimension=0, tiled=True)  113 us
    all_gather x1, waiting for transfers between devices, gather_rows(): return lax.all_gather(rows, 'blk', axis=0, tiled=True)  73.8 us
    all_gather x1, blocking collectives, sum_blocks(): lax.all_gather(lax.psum_scatter(terms, 'blk', scatter_dimension=0, tiled=...  44.9 us
    dot_general x13, matrix products, dot(): lax.dot_general(a, b, (((ca,), (cb,)), ((), ())), precision=precision, pr...  16.5 us
  transfers between devices with their start and end apart: 4, of which 3 were waited for; matrix products, arithmetic and copies ran while one was open for 2% of the time, Pallas kernels for 0%

profile of v1, /device:TPU:2, one launch (start us, length us, event | category | flops | bytes accessed | tf_op | source)
XLA Modules:
  0.0 490.5 jit_solution(10927316660636369088)
XLA Ops:
  7.3 1.0 compare_reduce_fusion.1
  8.2 0.8 compare_reduce_fusion
  9.2 0.9 broadcast_multiply_fusion.1
  10.1 1.2 convolution_subtract_fusion
  11.3 1.2 convolution_subtract_fusion.1
  12.5 0.7 pad_maximum_fusion.3
  13.2 73.8 %all-gather.3.cloned.1.call-done = f32[1024,1024]{1,0:T(8,128)} async-done(((f32[32,1024]{1,0:T(8,128)}), f32[1024,1024]{1,0:T(8,128)}) %all-gather.3.cloned.1.call-update) | async-done | bytes 4194320 | tf_op jit(solution)/shard_map/all_gather | solution.py:25
  87.0 7.0 %convolution_bitcast_fusion = f32[512,1024]{0,1:T(8,128)} fusion(f32[1024,1024]{1,0:T(8,128)} %all-gather.3.cloned.1.call-done, f32[1024,512]{1,0:T(8,128)S(1)} %copy-done), kind=kOutput, calls=%fused_computation | convolution fusion | flops 3221225472 | bytes 8388608 | tf_op jit(solution)/shard_map/dot_general | solution.py:12
  94.0 2.9 copy.11
  97.0 0.8 copy-done.4
  97.8 2.9 collective-permute-start
  100.7 210.4 %reduce-scatter.7.cloned.1.call-done = f32[32,1024]{1,0:T(8,128)} async-done(((f32[512,1024]{1,0:T(8,128)}), f32[32,1024]{1,0:T(8,128)}) %reduce-scatter.7.cloned.1.call-update) | async-done | bytes 131088
  311.1 1.1 copy.12
  314.3 1.3 pad_maximum_fusion
  315.7 1.3 fusion
  317.1 1.3 fusion.2
  318.4 1.3 convolution_bitcast_fusion.1
  319.7 1.3 convolution_bitcast_fusion.2
  321.0 1.0 broadcast_multiply_fusion
  322.1 1.9 copy.10
  323.9 113.0 %reduce-scatter.5.cloned.1.call-done = f32[48,256]{1,0:T(8,128)} async-done(((f32[1536,256]{1,0:T(8,128)}), f32[48,256]{1,0:T(8,128)}) %reduce-scatter.5.cloned.1.call-update) | async-done | bytes 49168 | tf_op jit(solution)/shard_map/reduce_scatter | solution.py:34
  437.0 44.9 %all-gather = f32[768,256]{1,0:T(8,128)S(1)} all-gather(f32[48,256]{1,0:T(8,128)} %reduce-scatter.5.cloned.1.call-done), channel_id=2, replica_groups=mesh['grp'=16,'blk'=32] {'grp'}, dimensions={0}, use_global_device_ids=true | all-gather | bytes 835584 | tf_op jit(solution)/shard_map/all_gather | solution.py:34
  481.9 0.6 fusion.32
  482.5 1.5 slice_add_fusion
  (34 shorter events, 2.6 us)
Async XLA Ops:
  7.2 79.8 %copy-start = (f32[1024,512]{1,0:T(8,128)S(1)}, f32[1024,512]{1,0:T(8,128)}, u32[]{:S(2)}) copy-start(f32[1024,512]{1,0:T(8,128)} %param.6) | copy-start | bytes 6291460
  7.2 79.8 %all-gather.3.cloned.1.call-start = ((), (), s32[]{:S(2)}) async-start(), calls=%async_computation.2 | async-start | bytes 4325376 | tf_op jit(solution)/shard_map/all_gather | solution.py:25
  13.2 297.9 %reduce-scatter.7.cloned.1.call-start = ((), (), s32[]{:S(2)}) async-start(), calls=%async_computation.4 | async-start | bytes 2228224
  96.9 0.9 copy-start.4
  96.9 340.0 %reduce-scatter.5.cloned.1.call-start = ((), (), s32[]{:S(2)}) async-start(), calls=%async_computation.3 | async-start | bytes 1622016 | tf_op jit(solution)/shard_map/reduce_scatter | solution.py:34
  97.8 214.3 %collective-permute-start = (f32[32,1024]{1,0:T(8,128)S(1)}, f32[32,1024]{1,0:T(8,128)S(1)}, u32[]{:S(2)}, u32[]{:S(2)}) collective-permute-start(f32[32,1024]{1,0:T(8,128)S(1)} %copy-done.4), channel_id=1, source_target_pairs={{0,0},{1,32},{2,64},{3,96},{4,128},{5,160},{6,192},{7,224},{8,256}... | collective-permute-start | bytes 393224 | tf_op jit(solution)/shard_map/ppermute | solution.py:49
  314.3 1.5 copy-start.1
  318.4 1.3 copy-start.2
  321.0 160.9 %copy-start.3 = (f32[256,256]{1,0:T(8,128)S(1)}, f32[256,256]{1,0:T(8,128)}, u32[]{:S(2)}) copy-start(f32[256,256]{1,0:T(8,128)} %copy-done.2) | copy-start | bytes 786436
Sparse Core Ops, SparseCore 0:
  13.3 73.6 all-gather.2
  97.1 213.9 reduce-scatter.6
  315.7 121.2 reduce-scatter.4
